TPU v7x, 512 devices: a whole 4x4x16 slice. The times are simulated.
512 devices in a mesh: gx: 32 (over y, x, core), vert: 16 (over z).
Axes of the slice: x: 4, y: 4, z: 16, core: 2. Of those that a mesh axis runs over, the one named last changes fastest.
Arguments:
- state: float32 [256, 16, 16384], P('gx', None, 'vert'), may hold values from -6 to 6
- macro: float32 [5, 256, 16], P(None, 'gx'), may hold values from -4 to 4
- relax_rate: float32 [256, 16], P('gx'), may hold values from 0.01 to 300, as said below
- velocity: float32 [3, 16384], P(None, 'vert'), may hold values from -2 to 4
- vel_sign: int32 [16384], P('vert'), may hold values from 0 to 1, as said below
- quad_weight: float32 [16384], P('vert'), may hold values from 0.5 to 2
- freestream: float32 [16, 16384], P(None, 'vert'), may hold values from -6 to 6
- wall_flag: int32 [16], replicated, may hold values 0 or 1
Outputs:
- new_state: float32 [256, 16, 16384], P('gx', None, 'vert')
- new_macro: float32 [5, 256, 16], P(None, 'gx')
Inputs may be any that keep to these rules, and one draw needn't show every extreme that they name: Each row of relax_rate varies from cell to cell. `vel_sign`: every aligned block of 1024 velocities holds both signs.
All inputs are finite; a program needn't handle non-finite values.
Results may differ from a plain program's by a relative error of at most 0.00013.
Values sent between devices are 32-bit elements; how exact they have to be, the bound alone decides.
No kernel may reach another device: no remote copies, remote signals or barrier semaphores. Data moves between devices by JAX's collectives and lax.ppermute only.
A program may use at most 64 MiB of HBM per device.

v0:
```python
import jax
import jax.numpy as jnp
from jax import lax
from jax.sharding import PartitionSpec as P

exact_mode = lax.Precision.HIGHEST


def prefix(value, axis, join, neutral, backward):
    count, mine = (lax.axis_size(axis), lax.axis_index(axis))
    pieces = jax.tree.map(lambda part: lax.all_gather(part, axis), value)
    if backward:
        pieces = jax.tree.map(lambda part: part[::-1], pieces)
        mine = count - 1 - mine
    total = jax.tree.map(
        lambda part, zero: jnp.full_like(part, 0) + jnp.asarray(zero, part.dtype), value, neutral
    )

    def turn(position, total):
        longer = join(total, jax.tree.map(lambda part: part[position], pieces))
        return jax.tree.map(lambda new, old: jnp.where(position < mine, new, old), longer, total)

    return lax.fori_loop(0, count - 1, turn, total)


def with_halo(cells, sides, width):
    for axis, dim in sides:
        count = lax.axis_size(axis)
        ends = count - 1
        head = lax.slice_in_dim(cells, 0, width, axis=dim)
        tail = lax.slice_in_dim(cells, cells.shape[dim] - width, cells.shape[dim], axis=dim)
        cells = jnp.concatenate(
            [
                lax.ppermute(tail, axis, [(i, (i + 1) % count) for i in range(ends)]),
                cells,
                lax.ppermute(head, axis, [((i + 1) % count, i) for i in range(ends)]),
            ],
            axis=dim,
        )
    return cells


def basis_sets(velocity, vel_sign, quad_weight, groups):
    magnitude = velocity[0]
    along_x = jnp.where(vel_sign == 1, magnitude, -magnitude)
    along_y = velocity[1]
    along_z = velocity[2]
    square = along_x * along_x + along_y * along_y + along_z * along_z
    ones_row = jnp.ones_like(along_x)
    equil_basis = jnp.stack([ones_row, 2.0 * along_x, 2.0 * along_y, 2.0 * along_z, square - 1.5])
    weights = quad_weight / (quad_weight.shape[0] * groups)
    heat_factor = 0.2 * (square - 2.5)
    moment_rows = jnp.stack(
        [
            ones_row,
            along_x,
            along_y,
            along_z,
            2.0 / 3.0 * square - 1.0,
            2.0 * along_x * along_y,
            2.0 * along_x * along_z,
            2.0 * along_y * along_z,
            2.0 * (along_x * along_x - square / 3.0),
            2.0 * (along_y * along_y - square / 3.0),
            heat_factor * along_x,
            heat_factor * along_y,
            heat_factor * along_z,
        ]
    )
    outflux = jnp.where(vel_sign == 0, weights * magnitude, 0.0)
    influx = jnp.where(vel_sign == 1, weights * magnitude, 0.0)
    return (magnitude, equil_basis, moment_rows * weights, outflux, influx)


def compose(earlier, latter):
    return (latter[0] * earlier[0], latter[0] * earlier[1] + latter[1])


def march_zero(decay, driven, reverse):

    def advance_cell(carried, pieces):
        zero_run = pieces[0] * carried[0] + pieces[1]
        product = pieces[0] * carried[1]
        return ((zero_run, product), (zero_run, product))

    initial = (jnp.zeros_like(driven[0]), jnp.ones_like(driven[0]))
    _, (zero_runs, products) = lax.scan(advance_cell, initial, (decay, driven), reverse=reverse)
    return (zero_runs, products)


def advance(padded, relax_cells):
    conserved = padded[:5]
    flow_x = jnp.stack(
        [
            padded[1],
            padded[0] + padded[4] + padded[8],
            padded[5],
            padded[6],
            2.0 / 3.0 * (padded[1] + padded[10]),
        ]
    )
    flow_y = jnp.stack(
        [
            padded[2],
            padded[5],
            padded[0] + padded[4] + padded[9],
            padded[7],
            2.0 / 3.0 * (padded[2] + padded[11]),
        ]
    )
    centre = conserved[:, 1:-1, 1:-1]
    laplace = (
        conserved[:, 2:, 1:-1]
        + conserved[:, :-2, 1:-1]
        + conserved[:, 1:-1, 2:]
        + conserved[:, 1:-1, :-2]
        - 4.0 * centre
    )
    divergence = (
        flow_x[:, 2:, 1:-1] - flow_x[:, :-2, 1:-1] + flow_y[:, 1:-1, 2:] - flow_y[:, 1:-1, :-2]
    )
    diffusivity = 0.2 / (1.0 + relax_cells)
    return (centre + diffusivity * laplace - 0.25 * divergence, centre)


def local(state, macro, relax_rate, velocity, vel_sign, quad_weight, freestream, wall_flag):
    cells_x = state.shape[0]
    cells_y = state.shape[1]
    vel_count = state.shape[2]
    slab_count = lax.axis_size("gx")
    slab_index = lax.axis_index("gx")
    magnitude, equil_basis, moment_basis, outflux, influx = basis_sets(
        velocity, vel_sign, quad_weight, lax.axis_size("vert")
    )
    courant = cells_x * slab_count * magnitude
    relax_cell = relax_rate[:, :, None]
    flat_macro = macro.reshape(macro.shape[0], cells_x * cells_y)
    equil_state = jnp.einsum("kc,kv->cv", flat_macro, equil_basis, precision=exact_mode).reshape(
        cells_x, cells_y, vel_count
    )
    source = state + relax_cell * equil_state
    wall_mask = wall_flag[:, None] == 1
    wall_in = jnp.sum(influx) / slab_count
    divisor = 1.0 + courant + relax_cell
    decay = courant / divisor
    driven = source / divisor
    back_runs, back_products = march_zero(decay, driven, True)
    fore_runs, fore_products = march_zero(decay, driven, False)
    ones_plane = jnp.ones((cells_y, vel_count), jnp.float32)
    zero_plane = jnp.zeros((cells_y, vel_count), jnp.float32)
    back_maps = prefix(
        (back_products[0], back_runs[0]), "gx", compose, (ones_plane, zero_plane), True
    )
    entry_back = back_maps[0] * freestream + back_maps[1]
    back = back_products * entry_back + back_runs
    at_anchor = slab_index == 0
    wall_out = jnp.where(at_anchor, jnp.dot(back[0], outflux, precision=exact_mode), 0.0)
    wall_out, wall_in = lax.psum((wall_out, wall_in), ("gx", "vert"))
    rho_wall = wall_out / wall_in
    inflow_left = jnp.where(wall_mask, rho_wall[:, None], freestream)
    fore_maps = prefix(
        (fore_products[-1], fore_runs[-1]), "gx", compose, (ones_plane, zero_plane), False
    )
    entry_fore = fore_maps[0] * inflow_left + fore_maps[1]
    fore = fore_products * entry_fore + fore_runs
    kinetic = jnp.where(vel_sign == 1, fore, back)
    flattened = kinetic.reshape(cells_x * cells_y, vel_count)
    partial_value = jnp.einsum("cv,kv->kc", flattened, moment_basis, precision=exact_mode).reshape(
        13, cells_x, cells_y
    )
    moments = lax.psum(partial_value, "vert")
    padded = with_halo(moments, (("gx", 1),), 1)
    padded = jnp.concatenate([padded[:, :, -1:], padded, padded[:, :, :1]], axis=2)
    updated, centre = advance(padded, relax_rate)
    change = updated - centre
    flat_change = change.reshape(change.shape[0], cells_x * cells_y)
    correction = jnp.einsum("kc,kv->cv", flat_change, equil_basis, precision=exact_mode).reshape(
        cells_x, cells_y, vel_count
    )
    return (kinetic + correction, updated)


def solution(mesh):
    return jax.shard_map(
        local,
        mesh=mesh,
        in_specs=(
            P("gx", None, "vert"),
            P(None, "gx", None),
            P("gx", None),
            P(None, "vert"),
            P("vert"),
            P("vert"),
            P(None, "vert"),
            P(),
        ),
        out_specs=(P("gx", None, "vert"), P(None, "gx", None)),
        check_vma=False,
    )
```

profile of v0, /device:TPU:7, one launch (start us, length us, event | category | flops | bytes accessed | tf_op | source)
XLA Modules:
  0.0 472.6 jit_solution(17301780224435400815)
XLA Ops:
  9.6 1.9 select_reduce_fusion
  12.1 1.2 add_divide_fusion
  19.7 58.5 %all-gather.9.cloned.1.call-done = f32[32,16,1024]{2,1,0:T(8,128)} async-done(((f32[1,16,1024]{2,1,0:T(8,128)}), f32[32,16,1024]{2,1,0:T(8,128)}) %all-gather.9.cloned.1.call-update) | async-done | bytes 2097168 | tf_op jit(solution)/shard_map/all_gather | solution.py:11
  78.2 1.7 rev.6
  79.9 59.8 %all-gather.11.cloned.1.call-done = f32[32,16,1024]{2,1,0:T(8,128)} async-done(((f32[1,16,1024]{2,1,0:T(8,128)}), f32[32,16,1024]{2,1,0:T(8,128)}) %all-gather.11.cloned.1.call-update) | async-done | bytes 2097168 | tf_op jit(solution)/shard_map/all_gather | solution.py:11
  139.6 3.2 rev.7
  142.9 28.3 %while.71 = (s32[]{:T(128)}, f32[16,1024]{1,0:T(8,128)S(1)}, f32[16,1024]{1,0:T(8,128)S(1)}, s32[]{:T(128)}, f32[32,16,1024]{2,1,0:T(8,128)S(1)}, /*index=5*/f32[32,16,1024]{2,1,0:T(8,128)}, s32[]{:T(128)}, s32[]{:T(128)}) while((s32[]{:T(128)}, f32[16,1024]{1,0:T(8,128)S(1)}, f32[16,1024]{1,0:T(8,128)S(1)}, s32[]{:T(128)}, ...), condition=%wide.region_7.8_spmd.clone, body=%wide.region_6.7_spmd.clone.sunk | while | flops 114692 | bytes 393325 | solution.py:23
  172.4 28.8 %all-gather.5.cloned.1.call-done = f32[32,16,1024]{2,1,0:T(8,128)} async-done(((f32[1,16,1024]{2,1,0:T(8,128)}), f32[32,16,1024]{2,1,0:T(8,128)}) %all-gather.5.cloned.1.call-update) | async-done | bytes 2097168 | tf_op jit(solution)/shard_map/all_gather | solution.py:11
  201.2 61.3 %all-gather.7.cloned.1.call-done = f32[32,16,1024]{2,1,0:T(8,128)} async-done(((f32[1,16,1024]{2,1,0:T(8,128)}), f32[32,16,1024]{2,1,0:T(8,128)}) %all-gather.7.cloned.1.call-update) | async-done | bytes 2097168 | tf_op jit(solution)/shard_map/all_gather | solution.py:11
  262.6 29.2 %while.70 = (s32[]{:T(128)}, f32[16,1024]{1,0:T(8,128)S(1)}, f32[16,1024]{1,0:T(8,128)S(1)}, s32[]{:T(128)}, f32[32,16,1024]{2,1,0:T(8,128)}, /*index=5*/f32[32,16,1024]{2,1,0:T(8,128)}, s32[]{:T(128)}, s32[]{:T(128)}) while((s32[]{:T(128)}, f32[16,1024]{1,0:T(8,128)S(1)}, f32[16,1024]{1,0:T(8,128)S(1)}, s32[]{:T(128)}, ...), condition=%wide.region_3.4_spmd.clone, body=%wide.region_2.3_spmd.clone.sunk | while | flops 114692 | bytes 393325 | solution.py:23
  263.5 0.9 fusion.39
  264.4 0.9 fusion.39
  265.4 0.9 fusion.39
  266.3 0.9 fusion.39
  267.3 0.9 fusion.39
  268.2 0.9 fusion.39
  269.2 0.9 fusion.39
  271.1 0.9 fusion.39
  272.9 0.9 fusion.39
  274.8 0.9 fusion.39
  283.3 0.9 fusion.39
  285.2 0.9 fusion.39
  287.1 0.9 fusion.39
  289.0 0.9 fusion.39
  290.9 0.9 fusion.39
  291.8 103.7 %all-reduce = (f32[16]{0:T(128)S(1)}, f32[]{:T(128)}) all-reduce(f32[16]{0:T(128)S(1)} %fusion.2, f32[]{:T(128)S(6)} %div.41), channel_id=1, replica_groups=mesh['gx'=32,'vert'=16] {'gx','vert'}, use_global_device_ids=true, to_apply=%region_8.9 | all-reduce | flops 17 | bytes 136 | tf_op jit(solution)/shard_map/psum | solution.py:158
  396.4 1.9 fusion.3
  398.4 40.2 %psum.23 = f32[13,8,16]{2,0,1:T(8,128)S(1)} all-reduce(f32[13,8,16]{2,0,1:T(8,128)S(1)} %fusion.3), channel_id=1, replica_groups=mesh['gx'=32,'vert'=16] {'vert'}, use_global_device_ids=true, to_apply=%region_11.12 | all-reduce | flops 1664 | bytes 13312 | tf_op jit(solution)/shard_map/psum | solution.py:171
  438.6 17.3 %collective-permute-start.1 = (f32[13,1,16]{2,0,1:T(8,128)S(1)}, f32[13,1,16]{2,0,1:T(8,128)S(1)}, u32[]{:S(2)}, u32[]{:S(2)}) collective-permute-start(f32[13,1,16]{2,0,1:T(8,128)S(1)} %get-tuple-element.544), channel_id=1, source_target_pairs={{0,16},{16,32},{32,48},{48,64},{64,80},{80,96},{96,112},{112,128},... | collective-permute-start | bytes 2504 | tf_op jit(solution)/shard_map/ppermute | solution.py:34
  455.9 1.9 collective-permute-start
  457.9 5.1 %collective-permute-done = f32[13,1,16]{2,0,1:T(8,128)S(1)} collective-permute-done((f32[13,1,16]{2,0,1:T(8,128)S(1)}, f32[13,1,16]{2,0,1:T(8,128)S(1)}, u32[]{:S(2)}, u32[]{:S(2)}) %collective-permute-start) | collective-permute-done | bytes 864 | tf_op jit(solution)/shard_map/ppermute | solution.py:36
  464.0 1.5 convolution_add_fusion
  (143 shorter events, 55.1 us)
Async XLA Ops:
  7.2 71.0 %all-gather.9.cloned.1.call-start = ((), (), s32[]{:S(2)}) async-start(), calls=%async_computation.2 | async-start | bytes 2162688 | tf_op jit(solution)/shard_map/all_gather | solution.py:11
  9.6 4.0 copy-start.7
  14.7 125.0 %all-gather.11.cloned.1.call-start = ((), (), s32[]{:S(2)}) async-start(), calls=%async_computation.3 | async-start | bytes 2162688 | tf_op jit(solution)/shard_map/all_gather | solution.py:11
  15.4 185.8 %all-gather.5.cloned.1.call-start = ((), (), s32[]{:S(2)}) async-start(), calls=%async_computation | async-start | bytes 2162688 | tf_op jit(solution)/shard_map/all_gather | solution.py:11
  15.5 2.1 copy-start.5
  15.5 2.2 copy-start.10
  16.2 3.5 copy-start
  16.2 3.5 copy-start.2
  16.9 245.7 %all-gather.7.cloned.1.call-start = ((), (), s32[]{:S(2)}) async-start(), calls=%async_computation.1 | async-start | bytes 2162688 | tf_op jit(solution)/shard_map/all_gather | solution.py:11
  171.2 225.0 %copy-start.4 = (f32[16,1024]{1,0:T(8,128)S(1)}, f32[16,1024]{1,0:T(8,128)}, u32[]{:S(2)}) copy-start(f32[16,1024]{1,0:T(8,128)} %param.22) | copy-start | bytes 196612
  171.2 225.0 %copy-start.9 = (pred[16]{0:T(512)(128)(4,1)S(1)}, pred[16]{0:T(512)(128)(4,1)}, u32[]{:S(2)}) copy-start(pred[16]{0:T(512)(128)(4,1)} %broadcast_compare_fusion.1) | copy-start | bytes 52
  172.1 224.2 %copy-start.1 = (f32[8,16,1024]{2,1,0:T(8,128)S(1)}, f32[8,16,1024]{2,1,0:T(8,128)}, u32[]{:S(2)}) copy-start(f32[8,16,1024]{2,1,0:T(8,128)} %copy-done) | copy-start | bytes 1572868
  172.1 224.2 %copy-start.3 = (f32[8,16,1024]{2,1,0:T(8,128)S(1)}, f32[8,16,1024]{2,1,0:T(8,128)}, u32[]{:S(2)}) copy-start(f32[8,16,1024]{2,1,0:T(8,128)} %copy-done.2) | copy-start | bytes 1572868
  172.1 224.2 %copy-start.8 = (pred[1024]{0:T(1024)(128)(4,1)S(1)}, pred[1024]{0:T(1024)(128)(4,1)}, u32[]{:S(2)}) copy-start(pred[1024]{0:T(1024)(128)(4,1)} %copy-done.7) | copy-start | bytes 3076
  291.8 164.1 %copy-start.6 = (f32[8,16]{1,0:T(8,128)S(1)}, f32[8,16]{1,0:T(8,128)}, u32[]{:S(2)}) copy-start(f32[8,16]{1,0:T(8,128)} %param.18) | copy-start | bytes 1540
  438.6 19.3 %collective-permute-start.1 = (f32[13,1,16]{2,0,1:T(8,128)S(1)}, f32[13,1,16]{2,0,1:T(8,128)S(1)}, u32[]{:S(2)}, u32[]{:S(2)}) collective-permute-start(f32[13,1,16]{2,0,1:T(8,128)S(1)} %get-tuple-element.544), channel_id=1, source_target_pairs={{0,16},{16,32},{32,48},{48,64},{64,80},{80,96},{96,112},{112,128},... | collective-permute-start | bytes 2504 | tf_op jit(solution)/shard_map/ppermute | solution.py:34
  455.9 7.1 %collective-permute-start = (f32[13,1,16]{2,0,1:T(8,128)S(1)}, f32[13,1,16]{2,0,1:T(8,128)S(1)}, u32[]{:S(2)}, u32[]{:S(2)}) collective-permute-start(f32[13,1,16]{2,0,1:T(8,128)S(1)} %get-tuple-element.543), channel_id=1, source_target_pairs={{16,0},{32,16},{48,32},{64,48},{80,64},{96,80},{112,96},{128,112},... | collective-permute-start | bytes 2504 | tf_op jit(solution)/shard_map/ppermute | solution.py:36
Sparse Core Ops, SparseCore 0:
  14.8 63.3 all-gather.8
  81.3 58.3 all-gather.10
  142.8 58.3 all-gather.4
  204.2 58.3 all-gather.6
where the time goes:
time: 476 us; the launch traced here: 473 us
  waiting for transfers between devices  214 us (45%)
  blocking collectives  144 us (30%)
  other arithmetic  64.6 us (14%)
  starting transfers between devices  19.4 us (4%)
  between operations  14.8 us (3%)
  local copies, waits for them, and re-layouts  10.4 us (2%)
    all_gather x4, waiting for transfers between devices, prefix(): pieces = jax.tree.map(lambda part: lax.all_gather(part, axis), value)  208 us
    psum x1, blocking collectives, local(): wall_out, wall_in = lax.psum((wall_out, wall_in), ('gx', 'vert'))  104 us
    select_n x62, other arithmetic, turn(): jnp.where(position < mine, new, old)  56.1 us
    psum x1, blocking collectives, local(): moments = lax.psum(partial_value, 'vert')  40.2 us
    ppermute x1, starting transfers between devices, with_halo(): lax.ppermute(tail, axis, [(i, (i + 1) % count) for i in range(ends)])  17.3 us
  transfers between devices with their start and end apart: 6, of which 5 were waited for; matrix products, arithmetic and copies ran while one was open for 8% of the time, Pallas kernels for 0%

commit v1 on v0

--- a/solution.py
+++ b/solution.py
@@ -168,7 +168,7 @@
     partial_value = jnp.einsum("cv,kv->kc", flattened, moment_basis, precision=exact_mode).reshape(
         13, cells_x, cells_y
     )
-    moments = lax.psum(partial_value, "vert")
+    moments = jnp.sum(lax.all_gather(partial_value, "vert"), axis=0)
     padded = with_halo(moments, (("gx", 1),), 1)
     padded = jnp.concatenate([padded[:, :, -1:], padded, padded[:, :, :1]], axis=2)
     updated, centre = advance(padded, relax_rate)

time: 476 us -> 453 us (0.952)
  blocking collectives: 144 us -> 129 us
  starting transfers between devices: 19.4 us -> 12.5 us
  waiting for transfers between devices: 214 us -> 209 us
    psum x1 -> x0, blocking collectives: 40.2 us -> none  [local(): moments = lax.psum(partial_value, 'vert')]
    all_gather x0 -> x1, blocking collectives: none -> 25.2 us  [local(): moments = jnp.sum(lax.all_gather(partial_value, 'vert'), axis=0)]
    ppermute x1, starting transfers between devices: 17.3 us -> 2.73 us  [with_halo(): lax.ppermute(tail, axis, [(i, (i + 1) % count) for i in range(ends)])]
    ppermute x1, starting transfers between devices: 1.92 us -> 9.61 us  [with_halo(): lax.ppermute(head, axis, [((i + 1) % count, i) for i in range(ends)])]
    ppermute x1, waiting for transfers between devices: 5.12 us -> 0.01 us  [with_halo(): lax.ppermute(head, axis, [((i + 1) % count, i) for i in range(ends)])]
where the time goes in v1:
time: 453 us; the launch traced here: 447 us
  waiting for transfers between devices  209 us (46%)
  blocking collectives  129 us (28%)
  other arithmetic  64.6 us (14%)
  between operations  14.8 us (3%)
  starting transfers between devices  12.5 us (3%)
  local copies, waits for them, and re-layouts  10.7 us (2%)
    all_gather x4, waiting for transfers between devices, prefix(): pieces = jax.tree.map(lambda part: lax.all_gather(part, axis), value)  208 us
    psum x1, blocking collectives, local(): wall_out, wall_in = lax.psum((wall_out, wall_in), ('gx', 'vert'))  104 us
    select_n x62, other arithmetic, turn(): jnp.where(position < mine, new, old)  56.1 us
    all_gather x1, blocking collectives, local(): moments = jnp.sum(lax.all_gather(partial_value, 'vert'), axis=0)  25.2 us
    ppermute x1, starting transfers between devices, with_halo(): lax.ppermute(head, axis, [((i + 1) % count, i) for i in range(ends)])  9.61 us
  transfers between devices with their start and end apart: 6, of which 5 were waited for; matrix products, arithmetic and copies ran while one was open for 8% of the time, Pallas kernels for 0%

profile of v1, /device:TPU:7, one launch (start us, length us, event | category | flops | bytes accessed | tf_op | source)
XLA Modules:
  0.0 446.9 jit_solution(17237649071136930633)
XLA Ops:
  9.6 1.9 select_reduce_fusion
  12.2 1.2 add_divide_fusion
  19.6 58.6 %all-gather.10.cloned.1.call-done = f32[32,16,1024]{2,1,0:T(8,128)} async-done(((f32[1,16,1024]{2,1,0:T(8,128)}), f32[32,16,1024]{2,1,0:T(8,128)}) %all-gather.10.cloned.1.call-update) | async-done | bytes 2097168 | tf_op jit(solution)/shard_map/all_gather | solution.py:11
  78.2 1.7 rev.6
  79.9 59.8 %all-gather.12.cloned.1.call-done = f32[32,16,1024]{2,1,0:T(8,128)} async-done(((f32[1,16,1024]{2,1,0:T(8,128)}), f32[32,16,1024]{2,1,0:T(8,128)}) %all-gather.12.cloned.1.call-update) | async-done | bytes 2097168 | tf_op jit(solution)/shard_map/all_gather | solution.py:11
  139.7 3.2 rev.7
  142.9 28.3 %while.71 = (s32[]{:T(128)}, f32[16,1024]{1,0:T(8,128)S(1)}, f32[16,1024]{1,0:T(8,128)S(1)}, s32[]{:T(128)}, f32[32,16,1024]{2,1,0:T(8,128)S(1)}, /*index=5*/f32[32,16,1024]{2,1,0:T(8,128)}, s32[]{:T(128)}, s32[]{:T(128)}) while((s32[]{:T(128)}, f32[16,1024]{1,0:T(8,128)S(1)}, f32[16,1024]{1,0:T(8,128)S(1)}, s32[]{:T(128)}, ...), condition=%wide.region_7.8_spmd.clone, body=%wide.region_6.7_spmd.clone.sunk | while | flops 114692 | bytes 393325 | solution.py:23
  172.4 28.8 %all-gather.6.cloned.1.call-done = f32[32,16,1024]{2,1,0:T(8,128)} async-done(((f32[1,16,1024]{2,1,0:T(8,128)}), f32[32,16,1024]{2,1,0:T(8,128)}) %all-gather.6.cloned.1.call-update) | async-done | bytes 2097168 | tf_op jit(solution)/shard_map/all_gather | solution.py:11
  201.2 61.3 %all-gather.8.cloned.1.call-done = f32[32,16,1024]{2,1,0:T(8,128)} async-done(((f32[1,16,1024]{2,1,0:T(8,128)}), f32[32,16,1024]{2,1,0:T(8,128)}) %all-gather.8.cloned.1.call-update) | async-done | bytes 2097168 | tf_op jit(solution)/shard_map/all_gather | solution.py:11
  262.6 29.2 %while.70 = (s32[]{:T(128)}, f32[16,1024]{1,0:T(8,128)S(1)}, f32[16,1024]{1,0:T(8,128)S(1)}, s32[]{:T(128)}, f32[32,16,1024]{2,1,0:T(8,128)}, /*index=5*/f32[32,16,1024]{2,1,0:T(8,128)}, s32[]{:T(128)}, s32[]{:T(128)}) while((s32[]{:T(128)}, f32[16,1024]{1,0:T(8,128)S(1)}, f32[16,1024]{1,0:T(8,128)S(1)}, s32[]{:T(128)}, ...), condition=%wide.region_3.4_spmd.clone, body=%wide.region_2.3_spmd.clone.sunk | while | flops 114692 | bytes 393325 | solution.py:23
  263.5 0.9 fusion.35
  264.5 0.9 fusion.35
  265.4 0.9 fusion.35
  266.3 0.9 fusion.35
  267.3 0.9 fusion.35
  268.2 0.9 fusion.35
  269.2 0.9 fusion.35
  270.1 0.9 fusion.35
  271.1 0.9 fusion.35
  273.0 0.9 fusion.35
  274.8 0.9 fusion.35
  276.7 0.9 fusion.35
  285.2 0.9 fusion.35
  287.1 0.9 fusion.35
  289.0 0.9 fusion.35
  290.9 0.9 fusion.35
  291.8 103.7 %all-reduce = (f32[16]{0:T(128)S(1)}, f32[]{:T(128)}) all-reduce(f32[16]{0:T(128)S(1)} %fusion.2, f32[]{:T(128)S(6)} %div.41), channel_id=1, replica_groups=mesh['gx'=32,'vert'=16] {'gx','vert'}, use_global_device_ids=true, to_apply=%region_8.9 | all-reduce | flops 17 | bytes 136 | tf_op jit(solution)/shard_map/psum | solution.py:158
  396.4 1.9 fusion.13
  398.4 25.2 %all-gather = f32[208,8,16]{2,1,0:T(8,128)S(1)} all-gather(f32[13,8,16]{2,1,0:T(8,128)S(1)} %copy.37), channel_id=2, replica_groups=mesh['gx'=32,'vert'=16] {'vert'}, dimensions={0}, use_global_device_ids=true | all-gather | bytes 113152 | tf_op jit(solution)/shard_map/all_gather | solution.py:171
  423.9 9.6 %collective-permute-start = (f32[13,1,16]{0,2,1:T(8,128)S(1)}, f32[13,1,16]{0,2,1:T(8,128)S(1)}, u32[]{:S(2)}, u32[]{:S(2)}) collective-permute-start(f32[13,1,16]{0,2,1:T(8,128)S(1)} %get-tuple-element.545), channel_id=1, source_target_pairs={{16,0},{32,16},{48,32},{64,48},{80,64},{96,80},{112,96},{128,112},... | collective-permute-start | bytes 2504 | tf_op jit(solution)/shard_map/ppermute | solution.py:36
  433.5 2.7 collective-permute-start.1
  438.1 1.5 convolution_add_fusion
  (142 shorter events, 55.3 us)
Async XLA Ops:
  7.2 71.0 %all-gather.10.cloned.1.call-start = ((), (), s32[]{:S(2)}) async-start(), calls=%async_computation.2 | async-start | bytes 2162688 | tf_op jit(solution)/shard_map/all_gather | solution.py:11
  9.6 4.0 copy-start.7
  14.7 125.0 %all-gather.12.cloned.1.call-start = ((), (), s32[]{:S(2)}) async-start(), calls=%async_computation.3 | async-start | bytes 2162688 | tf_op jit(solution)/shard_map/all_gather | solution.py:11
  15.4 185.8 %all-gather.6.cloned.1.call-start = ((), (), s32[]{:S(2)}) async-start(), calls=%async_computation | async-start | bytes 2162688 | tf_op jit(solution)/shard_map/all_gather | solution.py:11
  15.5 2.1 copy-start.5
  15.5 2.1 copy-start.10
  16.2 3.4 copy-start
  16.2 3.4 copy-start.2
  16.9 245.7 %all-gather.8.cloned.1.call-start = ((), (), s32[]{:S(2)}) async-start(), calls=%async_computation.1 | async-start | bytes 2162688 | tf_op jit(solution)/shard_map/all_gather | solution.py:11
  171.2 225.0 %copy-start.4 = (f32[16,1024]{1,0:T(8,128)S(1)}, f32[16,1024]{1,0:T(8,128)}, u32[]{:S(2)}) copy-start(f32[16,1024]{1,0:T(8,128)} %param.22) | copy-start | bytes 196612
  171.2 225.0 %copy-start.9 = (pred[16]{0:T(512)(128)(4,1)S(1)}, pred[16]{0:T(512)(128)(4,1)}, u32[]{:S(2)}) copy-start(pred[16]{0:T(512)(128)(4,1)} %broadcast_compare_fusion.1) | copy-start | bytes 52
  172.1 224.2 %copy-start.1 = (f32[8,16,1024]{2,1,0:T(8,128)S(1)}, f32[8,16,1024]{2,1,0:T(8,128)}, u32[]{:S(2)}) copy-start(f32[8,16,1024]{2,1,0:T(8,128)} %copy-done) | copy-start | bytes 1572868
  172.1 224.2 %copy-start.3 = (f32[8,16,1024]{2,1,0:T(8,128)S(1)}, f32[8,16,1024]{2,1,0:T(8,128)}, u32[]{:S(2)}) copy-start(f32[8,16,1024]{2,1,0:T(8,128)} %copy-done.2) | copy-start | bytes 1572868
  172.1 224.2 %copy-start.8 = (pred[1024]{0:T(1024)(128)(4,1)S(1)}, pred[1024]{0:T(1024)(128)(4,1)}, u32[]{:S(2)}) copy-start(pred[1024]{0:T(1024)(128)(4,1)} %copy-done.7) | copy-start | bytes 3076
  396.3 39.9 %copy-start.6 = (f32[8,16]{1,0:T(8,128)S(1)}, f32[8,16]{1,0:T(8,128)}, u32[]{:S(2)}) copy-start(f32[8,16]{1,0:T(8,128)} %param.18) | copy-start | bytes 1540
  423.9 12.4 %collective-permute-start = (f32[13,1,16]{0,2,1:T(8,128)S(1)}, f32[13,1,16]{0,2,1:T(8,128)S(1)}, u32[]{:S(2)}, u32[]{:S(2)}) collective-permute-start(f32[13,1,16]{0,2,1:T(8,128)S(1)} %get-tuple-element.545), channel_id=1, source_target_pairs={{16,0},{32,16},{48,32},{64,48},{80,64},{96,80},{112,96},{128,112},... | collective-permute-start | bytes 2504 | tf_op jit(solution)/shard_map/ppermute | solution.py:36
  433.5 3.5 collective-permute-start.1
Sparse Core Ops, SparseCore 0:
  14.8 63.3 all-gather.9
  81.3 58.3 all-gather.11
  142.8 58.3 all-gather.5
  204.2 58.3 all-gather.7
